TPU v7x, 32 devices: a whole 2x2x4 slice. The times are simulated.
32 devices in a mesh: seq: 4 (over y, core), shard: 8 (over z, x).
Axes of the slice: x: 2, y: 2, z: 4, core: 2. Of those that a mesh axis runs over, the one named last changes fastest.
Arguments:
- tokens: bfloat16 [8, 1024, 1024], P('shard', 'seq'), may hold values from -6 to 6
- doc_starts: int32 [8, 4], P('shard'), may hold values from 0 to 1023, as said below
- pre_gain: bfloat16 [1024], P('shard'), may hold values from 0.099609375 to 1.8984375
- query_weight: bfloat16 [1024, 1024], P('shard'), may hold values from -0.1875 to 0.1875
- key_matrix: bfloat16 [1024, 512], P('shard'), may hold values from -0.1875 to 0.1875
- value_matrix: bfloat16 [1024, 512], P('shard'), may hold values from -0.1875 to 0.1875
- query_gain: bfloat16 [64], P('shard'), may hold values from 0.099609375 to 1.8984375
- key_gain: bfloat16 [64], P('shard'), may hold values from 0.099609375 to 1.8984375
- out_weight: bfloat16 [1024, 1024], P('shard'), may hold values from -0.75 to 0.75
- post_gain: bfloat16 [1024], P('shard'), may hold values from 0.099609375 to 1.8984375
- gate_weight: bfloat16 [1024, 4608], P('shard'), may hold values from -0.1875 to 0.1875
- up_weight: bfloat16 [1024, 4608], P('shard'), may hold values from -0.1875 to 0.1875
- down_weight: bfloat16 [4608, 1024], P('shard'), may hold values from -0.09375 to 0.09375
- cotangent: bfloat16 [8, 1024, 1024], P('shard', 'seq'), may hold values from -6 to 6
Outputs:
- output: bfloat16 [8, 1024, 1024], P('shard', 'seq')
- grad_tokens: float32 [8, 1024, 1024], P('shard', 'seq')
- grad_pregain: float32 [1024], P('shard')
- grad_qweight: float32 [1024, 1024], P('shard')
- grad_kweight: float32 [1024, 512], P('shard')
- grad_vweight: float32 [1024, 512], P('shard')
- grad_qgain: float32 [64], P('shard')
- grad_kgain: float32 [64], P('shard')
- grad_oweight: float32 [1024, 1024], P('shard')
- grad_postgain: float32 [1024], P('shard')
- grad_gate: float32 [1024, 4608], P('shard')
- grad_up: float32 [1024, 4608], P('shard')
- grad_down: float32 [4608, 1024], P('shard')
Inputs may be any that keep to these rules, and one draw needn't show every extreme that they name: `doc_starts`: in each packed row the 4 document starts rise strictly; the first is 0.
All inputs are finite; a program needn't handle non-finite values.
Results may differ from a plain program's by a relative error of at most 0.023.
Values may be sent and summed in bfloat16 or wider, within the bound.
No kernel may reach another device: no remote copies, remote signals or barrier semaphores. Data moves between devices by JAX's collectives and lax.ppermute only.
A program may use at most 256 MiB of HBM per device.

v0:
```python
import math

import jax
import jax.numpy as jnp
from jax import lax
from jax.sharding import PartitionSpec as P

QUERY_HEADS = 16
KEY_VALUE_HEADS = 8
HEAD_SIZE = 64


eps_norm = 1e-05
rope_base = 1000000.0
masked_score = -1e30


def times_t(left, right):
    return lax.dot_general(
        left, right, (((1,), (1,)), ((), ())), preferred_element_type=jnp.float32
    )


def t_times(left, right):
    return lax.dot_general(
        left, right, (((0,), (0,)), ((), ())), preferred_element_type=jnp.float32
    )


def inverse_root(value_tokens):
    return lax.rsqrt(jnp.mean(value_tokens * value_tokens, axis=-1, keepdims=True) + eps_norm)


def norm_back(grad_scaled, value_tokens, root):
    return root * (
        grad_scaled
        - value_tokens
        * (root * root)
        * jnp.mean(grad_scaled * value_tokens, axis=-1, keepdims=True)
    )


def rope_tables(places):
    inverse = jnp.exp(
        jnp.arange(HEAD_SIZE // 2, dtype=jnp.float32) * (-2.0 * math.log(rope_base) / HEAD_SIZE)
    )
    angle = places.astype(jnp.float32)[:, None] * inverse[None, :]
    angle = jnp.concatenate([angle, angle], axis=1)
    return (jnp.cos(angle)[:, None, :], jnp.sin(angle)[:, None, :])


def rotate(value_tokens, cosine, sine):
    half = HEAD_SIZE // 2
    turned = jnp.concatenate([-value_tokens[..., half:], value_tokens[..., :half]], axis=-1)
    return value_tokens * cosine + turned * sine


def rotate_back(grads, cosine, sine):
    half = HEAD_SIZE // 2
    scaled = grads * sine
    return grads * cosine + jnp.concatenate([scaled[..., half:], -scaled[..., :half]], axis=-1)


def segment_info(starts, places):
    before = starts[None, :] <= places[:, None]
    segment = jnp.sum(before.astype(jnp.int32), axis=1)
    begin = jnp.max(jnp.where(before, starts[None, :], 0), axis=1)
    return (segment, places - begin)


def allowed_mask(segment, query_first, key_first, block):
    query_seg = lax.dynamic_slice_in_dim(segment, query_first, block, 0)
    key_seg = lax.dynamic_slice_in_dim(segment, key_first, block, 0)
    query_place = query_first + jnp.arange(block, dtype=jnp.int32)
    key_place = key_first + jnp.arange(block, dtype=jnp.int32)
    return (query_seg[:, None] == key_seg[None, :]) & (query_place[:, None] >= key_place[None, :])


def attend_item(query_pair, key_value, segment, block):
    length = query_pair.shape[0]
    head_group_size = query_pair.shape[1] // HEAD_SIZE
    queries = query_pair.reshape(length, head_group_size, HEAD_SIZE).transpose(1, 0, 2)
    key_tokens = key_value[:, :HEAD_SIZE]
    value_tokens = key_value[:, HEAD_SIZE:]
    scale = HEAD_SIZE ** (-0.5)

    def query_block(index):
        first = index * block
        query_rows = lax.dynamic_slice_in_dim(queries, first, block, 1)

        def key_step(inner, carry):
            running, total, summed = carry
            start = inner * block
            key_rows = lax.dynamic_slice_in_dim(key_tokens, start, block, 0)
            value_rows = lax.dynamic_slice_in_dim(value_tokens, start, block, 0)
            allowed = allowed_mask(segment, first, start, block)
            scores = (
                jnp.einsum("hqd,kd->hqk", query_rows, key_rows, preferred_element_type=jnp.float32)
                * scale
            )
            scores = jnp.where(allowed[None], scores, masked_score)
            highest = jnp.maximum(running, jnp.max(scores, axis=2))
            weights = jnp.exp(scores - highest[:, :, None])
            factor = jnp.exp(running - highest)
            total = total * factor + jnp.sum(weights, axis=2)
            summed = summed * factor[:, :, None] + jnp.einsum(
                "hqk,kd->hqd",
                weights.astype(jnp.bfloat16),
                value_rows,
                preferred_element_type=jnp.float32,
            )
            return (highest, total, summed)

        initial = (
            jnp.full((head_group_size, block), masked_score, jnp.float32),
            jnp.zeros((head_group_size, block), jnp.float32),
            jnp.zeros((head_group_size, block, HEAD_SIZE), jnp.float32),
        )
        running, total, summed = lax.fori_loop(0, index + 1, key_step, initial)
        return (summed / total[:, :, None], running + jnp.log(total))

    blocks_out, blocks_log = lax.map(query_block, jnp.arange(length // block, dtype=jnp.int32))
    attended = (
        blocks_out.transpose(0, 2, 1, 3)
        .reshape(length, head_group_size * HEAD_SIZE)
        .astype(jnp.bfloat16)
    )
    logsum = blocks_log.transpose(0, 2, 1).reshape(length, head_group_size)
    return (attended, logsum)


def attend_back(query_pair, key_value, grad_pair, delta, logsum, segment, block):
    length = query_pair.shape[0]
    head_group_size = query_pair.shape[1] // HEAD_SIZE
    queries = query_pair.reshape(length, head_group_size, HEAD_SIZE).transpose(1, 0, 2)
    grads_out = grad_pair.reshape(length, head_group_size, HEAD_SIZE).transpose(1, 0, 2)
    key_tokens = key_value[:, :HEAD_SIZE]
    value_tokens = key_value[:, HEAD_SIZE:]
    logsum_heads = logsum.T
    delta_heads = delta.T
    scale = HEAD_SIZE ** (-0.5)
    count = length // block

    def key_block(query_grad, index):
        start = index * block
        key_rows = lax.dynamic_slice_in_dim(key_tokens, start, block, 0)
        value_rows = lax.dynamic_slice_in_dim(value_tokens, start, block, 0)

        def query_step(inner, carry):
            key_grad, value_grad, query_grad = carry
            first = inner * block
            query_rows = lax.dynamic_slice_in_dim(queries, first, block, 1)
            grad_rows = lax.dynamic_slice_in_dim(grads_out, first, block, 1)
            log_rows = lax.dynamic_slice_in_dim(logsum_heads, first, block, 1)
            delta_rows = lax.dynamic_slice_in_dim(delta_heads, first, block, 1)
            allowed = allowed_mask(segment, first, start, block)
            scores = (
                jnp.einsum("hqd,kd->hqk", query_rows, key_rows, preferred_element_type=jnp.float32)
                * scale
            )
            scores = jnp.where(allowed[None], scores, masked_score)
            probs = jnp.exp(scores - log_rows[:, :, None])
            grad_probs = jnp.einsum(
                "hqd,kd->hqk", grad_rows, value_rows, preferred_element_type=jnp.float32
            )
            grad_scores = (probs * (grad_probs - delta_rows[:, :, None])).astype(jnp.bfloat16)
            value_grad = value_grad + jnp.einsum(
                "hqk,hqd->kd",
                probs.astype(jnp.bfloat16),
                grad_rows,
                preferred_element_type=jnp.float32,
            )
            key_grad = (
                key_grad
                + jnp.einsum(
                    "hqk,hqd->kd", grad_scores, query_rows, preferred_element_type=jnp.float32
                )
                * scale
            )
            addition = (
                jnp.einsum("hqk,kd->hqd", grad_scores, key_rows, preferred_element_type=jnp.float32)
                * scale
            )
            current = lax.dynamic_slice_in_dim(query_grad, first, block, 1)
            query_grad = lax.dynamic_update_slice_in_dim(query_grad, current + addition, first, 1)
            return (key_grad, value_grad, query_grad)

        zeros_block = jnp.zeros((block, HEAD_SIZE), jnp.float32)
        key_grad, value_grad, query_grad = lax.fori_loop(
            index, count, query_step, (zeros_block, zeros_block, query_grad)
        )
        return (query_grad, jnp.concatenate([key_grad, value_grad], axis=1))

    query_grad, pair_grads = lax.scan(
        key_block,
        jnp.zeros((head_group_size, length, HEAD_SIZE), jnp.float32),
        jnp.arange(count, dtype=jnp.int32),
    )
    query_grad = (
        query_grad.transpose(1, 0, 2)
        .reshape(length, head_group_size * HEAD_SIZE)
        .astype(jnp.bfloat16)
    )
    return (query_grad, pair_grads.reshape(length, 2 * HEAD_SIZE).astype(jnp.bfloat16))


def per_device(
    tokens,
    doc_starts,
    pre_gain,
    query_weight,
    key_matrix,
    value_matrix,
    query_gain,
    key_gain,
    out_weight,
    post_gain,
    gate_weight,
    up_weight,
    down_weight,
    cotangent,
):
    local = tokens[0].astype(jnp.float32)
    packed_rows = local.shape[0]
    length = packed_rows * lax.axis_size("seq")
    block = min(512, length)
    head_group_size = QUERY_HEADS // KEY_VALUE_HEADS
    starts = doc_starts[0]
    segment, _ = segment_info(starts, jnp.arange(length, dtype=jnp.int32))
    places = lax.axis_index("seq") * packed_rows + jnp.arange(packed_rows, dtype=jnp.int32)
    _, inside = segment_info(starts, places)
    cosine, sine = rope_tables(inside)
    full_pre, full_query, full_key, full_value, full_qgain, full_kgain, full_out = (
        lax.all_gather(pre_gain, "shard", axis=0, tiled=True),
        lax.all_gather(query_weight, "shard", axis=0, tiled=True),
        lax.all_gather(key_matrix, "shard", axis=0, tiled=True),
        lax.all_gather(value_matrix, "shard", axis=0, tiled=True),
        lax.all_gather(query_gain, "shard", axis=0, tiled=True),
        lax.all_gather(key_gain, "shard", axis=0, tiled=True),
        lax.all_gather(out_weight, "shard", axis=0, tiled=True),
    )
    root_in = inverse_root(local)
    normalized_input = (local * root_in * full_pre.astype(jnp.float32)).astype(jnp.bfloat16)
    query_proj = jnp.dot(normalized_input, full_query, preferred_element_type=jnp.float32).reshape(
        packed_rows, QUERY_HEADS, HEAD_SIZE
    )
    key_projected = jnp.dot(normalized_input, full_key, preferred_element_type=jnp.float32).reshape(
        packed_rows, KEY_VALUE_HEADS, HEAD_SIZE
    )
    value_low = (
        jnp.dot(normalized_input, full_value, preferred_element_type=jnp.float32)
        .astype(jnp.bfloat16)
        .reshape(packed_rows, KEY_VALUE_HEADS, HEAD_SIZE)
    )
    query_root = inverse_root(query_proj)
    key_root = inverse_root(key_projected)
    query_reduced = rotate(
        query_proj * query_root * full_qgain.astype(jnp.float32), cosine, sine
    ).astype(jnp.bfloat16)
    key_low = rotate(
        key_projected * key_root * full_kgain.astype(jnp.float32), cosine, sine
    ).astype(jnp.bfloat16)
    query_by_group = query_reduced.reshape(
        packed_rows, KEY_VALUE_HEADS, head_group_size * HEAD_SIZE
    )
    pair_grouped = jnp.concatenate([key_low, value_low], axis=2)
    query_heads, pair_heads = (
        lax.all_to_all(query_by_group, "seq", split_axis=1, concat_axis=0, tiled=True),
        lax.all_to_all(pair_grouped, "seq", split_axis=1, concat_axis=0, tiled=True),
    )

    def attend_one(query_pair, key_value):
        return attend_item(query_pair, key_value, segment, block)

    attended, logsum = jax.vmap(attend_one, in_axes=1, out_axes=1)(query_heads, pair_heads)
    attention_tokens = lax.all_to_all(
        attended, "seq", split_axis=0, concat_axis=1, tiled=True
    ).reshape(packed_rows, QUERY_HEADS * HEAD_SIZE)
    middle = local + jnp.dot(attention_tokens, full_out, preferred_element_type=jnp.float32)
    full_post, full_gate, full_up, full_down = (
        lax.all_gather(post_gain, "shard", axis=0, tiled=True),
        lax.all_gather(gate_weight, "shard", axis=0, tiled=True),
        lax.all_gather(up_weight, "shard", axis=0, tiled=True),
        lax.all_gather(down_weight, "shard", axis=0, tiled=True),
    )
    root_mid = inverse_root(middle)
    normed_mid = (middle * root_mid * full_post.astype(jnp.float32)).astype(jnp.bfloat16)
    gate = jnp.dot(normed_mid, full_gate, preferred_element_type=jnp.float32)
    upper = jnp.dot(normed_mid, full_up, preferred_element_type=jnp.float32)
    sigmoid = jax.nn.sigmoid(gate)
    swish = gate * sigmoid
    hidden = (swish * upper).astype(jnp.bfloat16)
    output = middle + jnp.dot(hidden, full_down, preferred_element_type=jnp.float32)
    grad_out = cotangent[0]
    full_post, full_gate, full_up, full_down = (
        lax.all_gather(post_gain, "shard", axis=0, tiled=True),
        lax.all_gather(gate_weight, "shard", axis=0, tiled=True),
        lax.all_gather(up_weight, "shard", axis=0, tiled=True),
        lax.all_gather(down_weight, "shard", axis=0, tiled=True),
    )
    term_down = t_times(hidden, grad_out)
    grad_hidden = times_t(grad_out, full_down)
    grad_gact = (grad_hidden * upper * (sigmoid * (1.0 + gate * (1.0 - sigmoid)))).astype(
        jnp.bfloat16
    )
    grad_upper = (grad_hidden * swish).astype(jnp.bfloat16)
    term_gate = t_times(normed_mid, grad_gact)
    term_up = t_times(normed_mid, grad_upper)
    grad_nmid = times_t(grad_gact, full_gate) + times_t(grad_upper, full_up)
    term_post = jnp.sum(grad_nmid * middle * root_mid, axis=0)
    grad_middle = grad_out.astype(jnp.float32) + norm_back(
        grad_nmid * full_post.astype(jnp.float32), middle, root_mid
    )
    shard_post, shard_gate, shard_up, shard_down = (
        lax.psum_scatter(
            term_post.astype(jnp.bfloat16), "shard", scatter_dimension=0, tiled=True
        ).astype(jnp.float32),
        lax.psum_scatter(
            term_gate.astype(jnp.bfloat16), "shard", scatter_dimension=0, tiled=True
        ).astype(jnp.float32),
        lax.psum_scatter(
            term_up.astype(jnp.bfloat16), "shard", scatter_dimension=0, tiled=True
        ).astype(jnp.float32),
        lax.psum_scatter(
            term_down.astype(jnp.bfloat16), "shard", scatter_dimension=0, tiled=True
        ).astype(jnp.float32),
    )
    full_pre, full_query, full_key, full_value, full_qgain, full_kgain, full_out = (
        lax.all_gather(pre_gain, "shard", axis=0, tiled=True),
        lax.all_gather(query_weight, "shard", axis=0, tiled=True),
        lax.all_gather(key_matrix, "shard", axis=0, tiled=True),
        lax.all_gather(value_matrix, "shard", axis=0, tiled=True),
        lax.all_gather(query_gain, "shard", axis=0, tiled=True),
        lax.all_gather(key_gain, "shard", axis=0, tiled=True),
        lax.all_gather(out_weight, "shard", axis=0, tiled=True),
    )
    grad_branch = grad_middle.astype(jnp.bfloat16)
    term_out = t_times(attention_tokens, grad_branch)
    attended_gradient = times_t(grad_branch, full_out).astype(jnp.bfloat16)
    grad_heads = lax.all_to_all(
        attended_gradient.reshape(packed_rows, KEY_VALUE_HEADS, head_group_size * HEAD_SIZE),
        "seq",
        split_axis=1,
        concat_axis=0,
        tiled=True,
    )
    items = grad_heads.shape[1]
    delta = jnp.sum(
        (attended.astype(jnp.float32) * grad_heads.astype(jnp.float32)).reshape(
            length, items, head_group_size, HEAD_SIZE
        ),
        axis=3,
    )

    def back_one(query_pair, key_value, grad_pair, delta_pair, logsum_pair):
        return attend_back(
            query_pair, key_value, grad_pair, delta_pair, logsum_pair, segment, block
        )

    query_back, pair_back = jax.vmap(back_one, in_axes=1, out_axes=1)(
        query_heads, pair_heads, grad_heads, delta, logsum
    )
    grad_qtokens, pairwise_gradient = (
        lax.all_to_all(query_back, "seq", split_axis=0, concat_axis=1, tiled=True),
        lax.all_to_all(pair_back, "seq", split_axis=0, concat_axis=1, tiled=True),
    )
    grad_qnorm = rotate_back(
        grad_qtokens.reshape(packed_rows, QUERY_HEADS, HEAD_SIZE).astype(jnp.float32), cosine, sine
    )
    grad_knorm = rotate_back(pairwise_gradient[:, :, :HEAD_SIZE].astype(jnp.float32), cosine, sine)
    value_gradient_rows = pairwise_gradient[:, :, HEAD_SIZE:].reshape(
        packed_rows, KEY_VALUE_HEADS * HEAD_SIZE
    )
    term_qgain = jnp.sum(grad_qnorm * query_proj * query_root, axis=(0, 1))
    term_kgain = jnp.sum(grad_knorm * key_projected * key_root, axis=(0, 1))
    grad_qproj = (
        norm_back(grad_qnorm * full_qgain.astype(jnp.float32), query_proj, query_root)
        .astype(jnp.bfloat16)
        .reshape(packed_rows, QUERY_HEADS * HEAD_SIZE)
    )
    grad_kproj = (
        norm_back(grad_knorm * full_kgain.astype(jnp.float32), key_projected, key_root)
        .astype(jnp.bfloat16)
        .reshape(packed_rows, KEY_VALUE_HEADS * HEAD_SIZE)
    )
    term_query = t_times(normalized_input, grad_qproj)
    term_key = t_times(normalized_input, grad_kproj)
    term_value = t_times(normalized_input, value_gradient_rows)
    grad_nin = (
        times_t(grad_qproj, full_query)
        + times_t(grad_kproj, full_key)
        + times_t(value_gradient_rows, full_value)
    )
    term_pre = jnp.sum(grad_nin * local * root_in, axis=0)
    grad_tokens = grad_middle + norm_back(grad_nin * full_pre.astype(jnp.float32), local, root_in)
    shard_pre, shard_query, shard_key, shard_value, shard_qgain, shard_kgain, shard_out = (
        lax.psum_scatter(
            term_pre.astype(jnp.bfloat16), "shard", scatter_dimension=0, tiled=True
        ).astype(jnp.float32),
        lax.psum_scatter(
            term_query.astype(jnp.bfloat16), "shard", scatter_dimension=0, tiled=True
        ).astype(jnp.float32),
        lax.psum_scatter(
            term_key.astype(jnp.bfloat16), "shard", scatter_dimension=0, tiled=True
        ).astype(jnp.float32),
        lax.psum_scatter(
            term_value.astype(jnp.bfloat16), "shard", scatter_dimension=0, tiled=True
        ).astype(jnp.float32),
        lax.psum_scatter(
            term_qgain.astype(jnp.bfloat16), "shard", scatter_dimension=0, tiled=True
        ).astype(jnp.float32),
        lax.psum_scatter(
            term_kgain.astype(jnp.bfloat16), "shard", scatter_dimension=0, tiled=True
        ).astype(jnp.float32),
        lax.psum_scatter(
            term_out.astype(jnp.bfloat16), "shard", scatter_dimension=0, tiled=True
        ).astype(jnp.float32),
    )
    summed = (
        lax.psum(shard_pre.astype(jnp.bfloat16), "seq").astype(jnp.float32),
        lax.psum(shard_query.astype(jnp.bfloat16), "seq").astype(jnp.float32),
        lax.psum(shard_key.astype(jnp.bfloat16), "seq").astype(jnp.float32),
        lax.psum(shard_value.astype(jnp.bfloat16), "seq").astype(jnp.float32),
        lax.psum(shard_qgain.astype(jnp.bfloat16), "seq").astype(jnp.float32),
        lax.psum(shard_kgain.astype(jnp.bfloat16), "seq").astype(jnp.float32),
        lax.psum(shard_out.astype(jnp.bfloat16), "seq").astype(jnp.float32),
        lax.psum(shard_post.astype(jnp.bfloat16), "seq").astype(jnp.float32),
        lax.psum(shard_gate.astype(jnp.bfloat16), "seq").astype(jnp.float32),
        lax.psum(shard_up.astype(jnp.bfloat16), "seq").astype(jnp.float32),
        lax.psum(shard_down.astype(jnp.bfloat16), "seq").astype(jnp.float32),
    )
    return (
        output.astype(jnp.bfloat16)[None],
        grad_tokens[None],
        summed[0],
        summed[1],
        summed[2],
        summed[3],
        summed[4],
        summed[5],
        summed[6],
        summed[7],
        summed[8],
        summed[9],
        summed[10],
    )


def solution(mesh):
    placed = (
        P("shard", "seq", None),
        P("shard", None),
        P("shard"),
        P("shard", None),
        P("shard", None),
        P("shard", None),
        P("shard"),
        P("shard"),
        P("shard", None),
        P("shard"),
        P("shard", None),
        P("shard", None),
        P("shard", None),
        P("shard", "seq", None),
    )
    return jax.shard_map(
        per_device,
        mesh=mesh,
        in_specs=placed,
        out_specs=(
            P("shard", "seq", None),
            P("shard", "seq", None),
            P("shard"),
            P("shard", None),
            P("shard", None),
            P("shard", None),
            P("shard"),
            P("shard"),
            P("shard", None),
            P("shard"),
            P("shard", None),
            P("shard", None),
            P("shard", None),
        ),
        check_vma=False,
    )
```

profile of v0, /device:TPU:0, one launch (start us, length us, event | category | flops | bytes accessed | tf_op | source)
XLA Modules:
  0.0 1612.5 jit_solution(13090858401140479732)
XLA Ops:
  11.2 22.3 %all-gather = bf16[8,1,128]{2,1,0:T(2,128)(2,1)S(1)} all-gather(bf16[1,1,128]{2,1,0:T(2,128)(2,1)} %bitcast.386), channel_id=1, replica_groups=mesh['seq'=4,'shard'=8] {'shard'}, dimensions={0}, use_global_device_ids=true | all-gather | bytes 2304 | tf_op jit(solution)/shard_map/all_gather | solution.py:234
  37.2 17.3 %all-reduce.7 = (bf16[64]{0:T(256)(128)(2,1)S(1)}, bf16[64]{0:T(256)(128)(2,1)S(1)}) all-reduce(bf16[64]{0:T(256)(128)(2,1)S(1)} %dynamic-update-slice.15, bf16[64]{0:T(256)(128)(2,1)S(1)} %dynamic-update-slice.16), channel_id=1, replica_groups=mesh['seq'=4,'shard'=8] {'shard'}, use_global_device_ids=true, to_apply=%add | all-reduce | flops 128 | bytes 512
  59.3 34.9 %all-gather.12.cloned.1.call-done = bf16[1024,512]{1,0:T(8,128)(2,1)} async-done(((bf16[128,512]{1,0:T(8,128)(2,1)}), bf16[1024,512]{1,0:T(8,128)(2,1)}) %all-gather.12.cloned.1.call-update) | async-done | bytes 1048592 | tf_op jit(solution)/shard_map/all_gather | solution.py:236
  102.4 42.1 %all-gather.10.cloned.1.call-done = bf16[1024,1024]{1,0:T(8,128)(2,1)} async-done(((bf16[128,1024]{1,0:T(8,128)(2,1)}), bf16[1024,1024]{1,0:T(8,128)(2,1)}) %all-gather.10.cloned.1.call-update) | async-done | bytes 2097168 | tf_op jit(solution)/shard_map/all_gather | solution.py:235
  155.9 6.8 all-to-all-done
  162.7 20.3 %while.68 = (s32[]{:T(128)}, bf16[2,2,2,512,64]{3,4,2,1,0:T(8,128)(2,1)}, f32[2,2,2,512]{3,2,1,0:T(2,128)S(1)}, s32[2]{0:T(128)S(1)}, bf16[2,2,1024,64]{2,3,1,0:...) while((s32[]{:T(128)}, ...), condition=%wide.region_10.11_spmd, body=%wide.region_5.10_spmd.sunk | while | flops 281156608 | bytes 21698280 | solution.py:122
  174.5 7.7 while.71
  189.7 18.1 %all-gather.1 = bf16[8,1,128]{2,1,0:T(2,128)(2,1)S(1)} all-gather(bf16[1,1,128]{2,1,0:T(2,128)(2,1)S(1)} %bitcast.387), channel_id=1, replica_groups=mesh['seq'=4,'shard'=8] {'shard'}, dimensions={0}, use_global_device_ids=true | all-gather | bytes 2304 | tf_op jit(solution)/shard_map/all_gather | solution.py:281
  212.8 120.3 %all-gather.18.cloned.1.call-done = bf16[1024,4608]{1,0:T(8,128)(2,1)} async-done(((bf16[128,4608]{1,0:T(8,128)(2,1)}), bf16[1024,4608]{1,0:T(8,128)(2,1)}) %all-gather.18.cloned.1.call-update) | async-done | bytes 9437200 | tf_op jit(solution)/shard_map/all_gather | solution.py:282
  333.2 7.9 fusion.103
  341.1 130.4 %all-gather.20.cloned.1.call-done = bf16[1024,4608]{1,0:T(8,128)(2,1)} async-done(((bf16[128,4608]{1,0:T(8,128)(2,1)}), bf16[1024,4608]{1,0:T(8,128)(2,1)}) %all-gather.20.cloned.1.call-update) | async-done | bytes 9437200 | tf_op jit(solution)/shard_map/all_gather | solution.py:283
  471.5 8.0 fusion.104
  479.4 130.5 %all-gather.22.cloned.1.call-done = bf16[4608,1024]{1,0:T(8,128)(2,1)} async-done(((bf16[576,1024]{1,0:T(8,128)(2,1)}), bf16[4608,1024]{1,0:T(8,128)(2,1)}) %all-gather.22.cloned.1.call-update) | async-done | bytes 9437200 | tf_op jit(solution)/shard_map/all_gather | solution.py:284
  610.0 13.3 multiply_convert_fusion.1
  623.3 6.9 fusion.105
  641.5 8.5 all-to-all-done.3
  653.0 63.3 %while.70 = (s32[]{:T(128)}, f32[2,2,1024,64]{2,3,1,0:T(8,128)S(1)}, bf16[2,2,512,128]{3,2,0,1:T(8,128)(2,1)}, s32[2]{0:T(128)S(1)}, bf16[2,1024,64]{1,2,0:T(8,1...) while((s32[]{:T(128)}, ...), condition=%wide.region_18.19_spmd, body=%wide.region_14.18_spmd.sunk | while | flops 683475968 | bytes 27735928 | solution.py:194
  654.6 38.5 %while.72 = (s32[]{:T(128)}, f32[2,512,64]{1,2,0:T(8,128)S(1)}, f32[2,512,64]{1,2,0:T(8,128)S(1)}, f32[2,2,1024,64]{2,3,1,0:T(8,128)S(1)}, s32[1024]{0:T(1024)S(...) while((s32[]{:T(128)}, f32[2,512,64]{1,2,0:T(8,128)S(1)}, ...), condition=%wide.region_17.17_spmd, body=%wide.region_15.16_spmd.sunk | while | flops 682951680 | bytes 24847756 | solution.py:189
  695.8 19.5 %while.72 = (s32[]{:T(128)}, f32[2,512,64]{1,2,0:T(8,128)S(1)}, f32[2,512,64]{1,2,0:T(8,128)S(1)}, f32[2,2,1024,64]{2,3,1,0:T(8,128)S(1)}, s32[1024]{0:T(1024)S(...) while((s32[]{:T(128)}, f32[2,512,64]{1,2,0:T(8,128)S(1)}, ...), condition=%wide.region_17.17_spmd, body=%wide.region_15.16_spmd.sunk | while | flops 682951680 | bytes 24847756 | solution.py:189
  717.9 11.4 all_to_all.96
  742.3 11.5 all_to_all.97
  778.4 7.0 convolution_convert_fusion
  786.8 9.8 reduce-scatter.10.cloned.1.call-done
  796.7 66.1 %reduce-scatter.12.cloned.1.call-done = bf16[128,512]{1,0:T(8,128)(2,1)} async-done(((bf16[1024,512]{1,0:T(8,128)(2,1)}), bf16[128,512]{1,0:T(8,128)(2,1)}) %reduce-scatter.12.cloned.1.call-update) | async-done | bytes 131088 | tf_op jit(solution)/shard_map/reduce_scatter | solution.py:406
  862.8 70.1 %reduce-scatter.14.cloned.1.call-done = bf16[128,1024]{1,0:T(8,128)(2,1)} async-done(((bf16[1024,1024]{1,0:T(8,128)(2,1)}), bf16[128,1024]{1,0:T(8,128)(2,1)}) %reduce-scatter.14.cloned.1.call-update) | async-done | bytes 262160 | tf_op jit(solution)/shard_map/reduce_scatter | solution.py:415
  932.9 70.3 %reduce-scatter.8.cloned.1.call-done = bf16[128,1024]{1,0:T(8,128)(2,1)} async-done(((bf16[1024,1024]{1,0:T(8,128)(2,1)}), bf16[128,1024]{1,0:T(8,128)(2,1)}) %reduce-scatter.8.cloned.1.call-update) | async-done | bytes 262160 | tf_op jit(solution)/shard_map/reduce_scatter | solution.py:400
  1003.2 166.0 %reduce-scatter.16.cloned.1.call-done = bf16[128,4608]{1,0:T(8,128)(2,1)} async-done(((bf16[1024,4608]{1,0:T(8,128)(2,1)}), bf16[128,4608]{1,0:T(8,128)(2,1)}) %reduce-scatter.16.cloned.1.call-update) | async-done | bytes 1179664 | tf_op jit(solution)/shard_map/reduce_scatter | solution.py:318
  1169.3 166.2 %reduce-scatter.18.cloned.1.call-done = bf16[128,4608]{1,0:T(8,128)(2,1)} async-done(((bf16[1024,4608]{1,0:T(8,128)(2,1)}), bf16[128,4608]{1,0:T(8,128)(2,1)}) %reduce-scatter.18.cloned.1.call-update) | async-done | bytes 1179664 | tf_op jit(solution)/shard_map/reduce_scatter | solution.py:321
  1335.5 166.0 %reduce-scatter.20.cloned.1.call-done = bf16[576,1024]{1,0:T(8,128)(2,1)} async-done(((bf16[4608,1024]{1,0:T(8,128)(2,1)}), bf16[576,1024]{1,0:T(8,128)(2,1)}) %reduce-scatter.20.cloned.1.call-update) | async-done | bytes 1179664 | tf_op jit(solution)/shard_map/reduce_scatter | solution.py:324
  1501.6 7.9 fusion.55
  1512.0 19.6 %all-reduce.6 = (bf16[1024]{0:T(1024)(128)(2,1)S(1)}, bf16[64]{0:T(256)(128)(2,1)S(1)}, bf16[64]{0:T(256)(128)(2,1)S(1)}, bf16[1024]{0:T(1024)(128)(2,1)S(1)}) all-reduce(bf16[1024]{0:T(1024)(128)(2,1)S(1)} %get-tuple-element.523, bf16[64]{0:T(256)(128)(2,1)S(1)} %get-tuple-element.519, ...), channel_id=2, replica_groups=mesh['seq'=4,'shard'=8] {'shard'}, use_global_device_ids=true, to_apply=%region_23.24.clone | all-reduce | flops 2176 | bytes 8704
  1541.9 50.4 %all-reduce.12.cloned.1.call-done = (bf16[128,1024]{1,0:T(8,128)(2,1)}, bf16[128,512]{1,0:T(8,128)(2,1)}, bf16[128,512]{1,0:T(8,128)(2,1)}, bf16[128,1024]{1,0:T...) async-done(((bf16[128,1024]{1,0:T(8,128)(2,1)}, bf16[128,512]{1,0:T(8,128)(2,1)}, bf16[128,512]{1,0:T(8,128)(2,1)}, ...) | async-done | bytes 4325392 | tf_op jit(solution)/shard_map/psum | solution.py:421
  (391 shorter events, 197.7 us)
Async XLA Ops:
  7.2 50.1 %all-gather.14.cloned.1.call-start = ((), (), s32[]{:S(2)}) async-start(), calls=%async_computation.15 | async-start | bytes 1179648 | tf_op jit(solution)/shard_map/all_gather | solution.py:237
  7.9 86.3 %all-gather.12.cloned.1.call-start = ((), (), s32[]{:S(2)}) async-start(), calls=%async_computation.14 | async-start | bytes 1179648 | tf_op jit(solution)/shard_map/all_gather | solution.py:236
  8.7 135.8 %all-gather.10.cloned.1.call-start = ((), (), s32[]{:S(2)}) async-start(), calls=%async_computation.13 | async-start | bytes 2359296 | tf_op jit(solution)/shard_map/all_gather | solution.py:235
  9.4 86.3 %copy-start = (bf16[1,256,1024]{2,1,0:T(8,128)(2,1)S(1)}, bf16[1,256,1024]{2,1,0:T(8,128)(2,1)}, u32[]{:S(2)}) copy-start(bf16[1,256,1024]{2,1,0:T(8,128)(2,1)} %param.24) | copy-start | bytes 1572868
  9.4 200.6 %all-gather.16.cloned.1.call-start = ((), (), s32[]{:S(2)}) async-start(), calls=%async_computation.16 | async-start | bytes 2359296 | tf_op jit(solution)/shard_map/all_gather | solution.py:240
  10.0 323.2 %all-gather.18.cloned.1.call-start = ((), (), s32[]{:S(2)}) async-start(), calls=%async_computation.17 | async-start | bytes 10616832 | tf_op jit(solution)/shard_map/all_gather | solution.py:282
  10.6 460.9 %all-gather.20.cloned.1.call-start = ((), (), s32[]{:S(2)}) async-start(), calls=%async_computation.18 | async-start | bytes 10616832 | tf_op jit(solution)/shard_map/all_gather | solution.py:283
  33.5 113.9 %copy-start.46 = (f32[8,1,128]{2,1,0:T(1,128)}, f32[8,1,128]{2,1,0:T(1,128)S(1)}, u32[]{:S(2)}) copy-start(f32[8,1,128]{2,1,0:T(1,128)S(1)} %convert_element_type.308) | copy-start | bytes 12292
  54.5 94.7 %copy-start.53 = (f32[64]{0:T(128)}, f32[64]{0:T(128)S(1)}, u32[]{:S(2)}) copy-start(f32[64]{0:T(128)S(1)} %convert_element_type.247) | copy-start | bytes 772
  54.5 42.7 %copy-start.55 = (f32[64]{0:T(128)}, f32[64]{0:T(128)S(1)}, u32[]{:S(2)}) copy-start(f32[64]{0:T(128)S(1)} %convert_element_type.251) | copy-start | bytes 772
  55.5 93.7 %copy-start.25 = (f32[256,64]{0,1:T(8,128)}, f32[256,64]{0,1:T(8,128)S(1)}, u32[]{:S(2)}) copy-start(f32[256,64]{0,1:T(8,128)S(1)} %get-tuple-element.654) | copy-start | bytes 196612
  55.5 93.7 %copy-start.33 = (f32[256,64]{0,1:T(8,128)}, f32[256,64]{0,1:T(8,128)S(1)}, u32[]{:S(2)}) copy-start(f32[256,64]{0,1:T(8,128)S(1)} %get-tuple-element.655) | copy-start | bytes 196612
  57.3 90.0 %copy-start.50 = (f32[256]{0:T(256)}, f32[256]{0:T(256)S(1)}, u32[]{:S(2)}) copy-start(f32[256]{0:T(256)S(1)} %get-tuple-element.661) | copy-start | bytes 3076
  97.0 50.3 %copy-start.44 = (f32[256,8]{0,1:T(8,128)}, f32[256,8]{0,1:T(8,128)S(1)}, u32[]{:S(2)}) copy-start(f32[256,8]{0,1:T(8,128)S(1)} %get-tuple-element.659) | copy-start | bytes 24580
  98.2 52.1 %all-to-all-start.1 = ((bf16[256,8,128]{0,2,1:T(8,128)(2,1)}), bf16[256,8,128]{0,2,1:T(8,128)(2,1)}, u32[]{:S(2)}, u32[]{:S(2)}) async-start(bf16[256,8,128]{0,2,1:T(8,128)(2,1)} %pad_maximum_fusion), calls=%async_computation.1 | async-start | bytes 1048576 | tf_op jit(solution)/shard_map/all_to_all | solution.py:269
  150.3 12.3 all-to-all-start
  153.8 456.1 %all-gather.22.cloned.1.call-start = ((), (), s32[]{:S(2)}) async-start(), calls=%async_computation.19 | async-start | bytes 10616832 | tf_op jit(solution)/shard_map/all_gather | solution.py:284
  186.3 21.6 %all-to-all-start.2 = ((bf16[1024,2,128]{2,1,0:T(2,128)(2,1)}), bf16[1024,2,128]{2,1,0:T(2,128)(2,1)S(1)}, u32[]{:S(2)}, u32[]{:S(2)}) async-start(bf16[1024,2,128]{2,1,0:T(2,128)(2,1)} %copy.108), calls=%async_computation.2 | async-start | bytes 1048576 | tf_op jit(solution)/shard_map/all_to_all | solution.py:276
  212.6 422.2 %copy-start.8 = (f32[256,1024]{1,0:T(8,128)}, f32[256,1024]{1,0:T(8,128)S(1)}, u32[]{:S(2)}) copy-start(f32[256,1024]{1,0:T(8,128)S(1)} %get-tuple-element.671) | copy-start | bytes 3145732
  212.8 258.7 %copy-start.6 = (bf16[256,1024]{1,0:T(8,128)(2,1)}, bf16[256,1024]{1,0:T(8,128)(2,1)S(1)}, u32[]{:S(2)}) copy-start(bf16[256,1024]{1,0:T(8,128)(2,1)S(1)} %multiply_convert_fusion.5) | copy-start | bytes 1572868
  341.1 268.9 %copy-start.31 = (bf16[1,256,1024]{2,1,0:T(8,128)(2,1)S(1)}, bf16[1,256,1024]{2,1,0:T(8,128)(2,1)}, u32[]{:S(2)}) copy-start(bf16[1,256,1024]{2,1,0:T(8,128)(2,1)} %param.37) | copy-start | bytes 1572868
  637.8 12.3 all-to-all-start.3
  641.3 155.4 %reduce-scatter.10.cloned.1.call-start = ((), (), s32[]{:S(2)}) async-start(), calls=%async_computation.21 | async-start | bytes 1179648 | tf_op jit(solution)/shard_map/reduce_scatter | solution.py:403
  735.9 126.9 %reduce-scatter.12.cloned.1.call-start = ((), (), s32[]{:S(2)}) async-start(), calls=%async_computation.22 | async-start | bytes 1179648 | tf_op jit(solution)/shard_map/reduce_scatter | solution.py:406
  738.5 194.4 %reduce-scatter.14.cloned.1.call-start = ((), (), s32[]{:S(2)}) async-start(), calls=%async_computation.23 | async-start | bytes 2359296 | tf_op jit(solution)/shard_map/reduce_scatter | solution.py:415
  741.7 261.5 %reduce-scatter.8.cloned.1.call-start = ((), (), s32[]{:S(2)}) async-start(), calls=%async_computation.20 | async-start | bytes 2359296 | tf_op jit(solution)/shard_map/reduce_scatter | solution.py:400
  763.6 405.6 %reduce-scatter.16.cloned.1.call-start = ((), (), s32[]{:S(2)}) async-start(), calls=%async_computation.24 | async-start | bytes 10616832 | tf_op jit(solution)/shard_map/reduce_scatter | solution.py:318
  770.5 565.0 %reduce-scatter.18.cloned.1.call-start = ((), (), s32[]{:S(2)}) async-start(), calls=%async_computation.25 | async-start | bytes 10616832 | tf_op jit(solution)/shard_map/reduce_scatter | solution.py:321
  777.4 724.1 %reduce-scatter.20.cloned.1.call-start = ((), (), s32[]{:S(2)}) async-start(), calls=%async_computation.26 | async-start | bytes 10616832 | tf_op jit(solution)/shard_map/reduce_scatter | solution.py:324
  785.4 716.2 %copy-start.9 = (f32[256,1024]{1,0:T(8,128)S(1)}, f32[256,1024]{1,0:T(8,128)}, u32[]{:S(2)}) copy-start(f32[256,1024]{1,0:T(8,128)} %copy-done.8) | copy-start | bytes 3145732
  785.4 806.8 %all-reduce.12.cloned.1.call-start = ((), (), s32[]{:S(2)}) async-start(), calls=%async_computation.27 | async-start | bytes 8650752 | tf_op jit(solution)/shard_map/psum | solution.py:421
  1510.8 29.8 %copy-start.57 = (f32[256]{0:T(256)S(1)}, f32[256]{0:T(256)}, u32[]{:S(2)}) copy-start(f32[256]{0:T(256)} %get-tuple-element.660) | copy-start | bytes 3076
  (51 other events, 384.3 us)
Sparse Core Ops, SparseCore 0:
  10.1 43.0 all-gather.13
  55.3 38.8 all-gather.11
  96.4 48.0 all-gather.9
  146.4 47.3 all-gather.15
  195.9 137.2 all-gather.17
  335.2 136.2 all-gather.19
  473.7 136.2 all-gather.21
  736.0 60.6 reduce-scatter.9
  800.4 62.3 reduce-scatter.11
  866.2 66.6 reduce-scatter.13
  936.4 66.7 reduce-scatter.7
  1006.7 162.5 reduce-scatter.15
  1172.9 162.5 reduce-scatter.17
  1338.9 162.5 reduce-scatter.19
  1504.2 87.9 all-reduce.11
where the time goes:
time: 1620 us; the launch traced here: 1610 us
  waiting for transfers between devices  1240 us (77%)
  matrix products  127 us (8%)
  blocking collectives  107 us (7%)
  local copies, waits for them, and re-layouts  51.3 us (3%)
  other arithmetic  39.6 us (2%)
  between operations  17.4 us (1%)
    reduce_scatter x1, waiting for transfers between devices, per_device(): lax.psum_scatter(term_up.astype(jnp.bfloat16), 'shard', scatter_dimension...  166 us
    reduce_scatter x1, waiting for transfers between devices, per_device(): lax.psum_scatter(term_down.astype(jnp.bfloat16), 'shard', scatter_dimensi...  166 us
    reduce_scatter x1, waiting for transfers between devices, per_device(): lax.psum_scatter(term_gate.astype(jnp.bfloat16), 'shard', scatter_dimensi...  166 us
    all_gather x1, waiting for transfers between devices, per_device(): lax.all_gather(down_weight, 'shard', axis=0, tiled=True)  131 us
    all_gather x1, waiting for transfers between devices, per_device(): lax.all_gather(up_weight, 'shard', axis=0, tiled=True)  130 us
    all_gather x1, waiting for transfers between devices, per_device(): lax.all_gather(gate_weight, 'shard', axis=0, tiled=True)  120 us
    reduce_scatter x1, waiting for transfers between devices, per_device(): lax.psum_scatter(term_query.astype(jnp.bfloat16), 'shard', scatter_dimens...  70.3 us
    reduce_scatter x1, waiting for transfers between devices, per_device(): lax.psum_scatter(term_out.astype(jnp.bfloat16), 'shard', scatter_dimensio...  70.1 us
  transfers between devices with their start and end apart: 19, of which 15 were waited for; matrix products, arithmetic and copies ran while one was open for 7% of the time, Pallas kernels for 0%

commit v1 on v0

v1 whole, which is shorter than its diff:
```python
import math

import jax
import jax.numpy as jnp
from jax import lax
from jax.sharding import PartitionSpec as P

QUERY_HEADS = 16
KEY_VALUE_HEADS = 8
HEAD_SIZE = 64
GROUP = QUERY_HEADS // KEY_VALUE_HEADS


eps_norm = 1e-05
rope_base = 1000000.0
masked_score = -1e30

bf16 = jnp.bfloat16
f32 = jnp.float32


def dot(left, right):
    return jnp.dot(left, right, preferred_element_type=f32)


def times_t(left, right):
    return lax.dot_general(left, right, (((1,), (1,)), ((), ())), preferred_element_type=f32)


def t_times(left, right):
    return lax.dot_general(left, right, (((0,), (0,)), ((), ())), preferred_element_type=f32)


def inverse_root(value_tokens):
    return lax.rsqrt(jnp.mean(value_tokens * value_tokens, axis=-1, keepdims=True) + eps_norm)


def norm_back(grad_scaled, value_tokens, root):
    return root * (
        grad_scaled
        - value_tokens
        * (root * root)
        * jnp.mean(grad_scaled * value_tokens, axis=-1, keepdims=True)
    )


def rope_tables(places):
    inverse = jnp.exp(
        jnp.arange(HEAD_SIZE // 2, dtype=f32) * (-2.0 * math.log(rope_base) / HEAD_SIZE)
    )
    angle = places.astype(f32)[:, None] * inverse[None, :]
    angle = jnp.concatenate([angle, angle], axis=1)
    return (jnp.cos(angle)[:, None, :], jnp.sin(angle)[:, None, :])


def rotate(value_tokens, cosine, sine):
    half = HEAD_SIZE // 2
    turned = jnp.concatenate([-value_tokens[..., half:], value_tokens[..., :half]], axis=-1)
    return value_tokens * cosine + turned * sine


def rotate_back(grads, cosine, sine):
    half = HEAD_SIZE // 2
    scaled = grads * sine
    return grads * cosine + jnp.concatenate([scaled[..., half:], -scaled[..., :half]], axis=-1)


def segment_info(starts, places):
    before = starts[None, :] <= places[:, None]
    segment = jnp.sum(before.astype(jnp.int32), axis=1)
    begin = jnp.max(jnp.where(before, starts[None, :], 0), axis=1)
    return (segment, places - begin)


def per_device(
    tokens,
    doc_starts,
    pre_gain,
    query_weight,
    key_matrix,
    value_matrix,
    query_gain,
    key_gain,
    out_weight,
    post_gain,
    gate_weight,
    up_weight,
    down_weight,
    cotangent,
):
    S = lax.axis_size("seq")
    N = lax.axis_size("shard")
    Q = lax.axis_index("seq")
    T, D = tokens.shape[1:]
    L = S * T
    rows_d = D // N
    qd = QUERY_HEADS * HEAD_SIZE // S
    kd = KEY_VALUE_HEADS * HEAD_SIZE // S
    FF = gate_weight.shape[1]
    piece = FF // N // S
    FQ = FF // S

    def swap(x, step):
        return lax.ppermute(x, "seq", [(i, i ^ step) for i in range(S)])

    def gather_seq(x):
        blocks = x[None]
        step = S // 2
        while step:
            other = swap(blocks, step)
            blocks = jnp.stack([blocks, other], axis=1).reshape((-1,) + x.shape)
            step //= 2
        return blocks

    def gather_rows(x):
        return gather_seq(x).reshape((-1,) + x.shape[1:])

    def scatter_seq(rows):
        def reduce(low, size):
            if size == 2:
                both = rows(low * T, 2 * T)
                return both[:T] + swap(both[T:].astype(bf16), 1).astype(f32)
            half = size // 2
            far = swap(reduce(low + half, half).astype(bf16), half)
            return reduce(low, half) + far.astype(f32)

        return reduce(0, S)

    def order_seq(blocks):
        return jnp.stack([lax.dynamic_index_in_dim(blocks, Q ^ i, 0, False) for i in range(S)])

    starts = doc_starts[0]
    blocks_at = jnp.arange(S, dtype=jnp.int32) ^ Q
    places = (blocks_at[:, None] * T + jnp.arange(T, dtype=jnp.int32)[None, :]).reshape(L)
    segment, inside = segment_info(starts, places)
    cosine, sine = rope_tables(inside)
    allowed = (segment[:, None] == segment[None, :]) & (places[:, None] >= places[None, :])

    width = qd + 2 * kd
    own = jnp.concatenate(
        [
            lax.dynamic_slice_in_dim(query_weight, Q * qd, qd, 1),
            lax.dynamic_slice_in_dim(key_matrix, Q * kd, kd, 1),
            lax.dynamic_slice_in_dim(value_matrix, Q * kd, kd, 1),
            lax.dynamic_slice_in_dim(out_weight, Q * (D // S), D // S, 1),
        ],
        axis=1,
    )
    gains = jnp.concatenate([pre_gain, post_gain, query_gain, key_gain])
    gains_rows = jnp.zeros((16, own.shape[1]), bf16)
    gains_rows = gains_rows.at[0, : gains.shape[0]].set(gains)
    packed = lax.all_gather(jnp.concatenate([own, gains_rows], axis=0), "shard", axis=0)
    full_qkv = packed[:, :rows_d, :width].reshape(D, width)
    out_columns = packed[:, :rows_d, width:].reshape(D, D // S)
    full_gains = packed[:, rows_d, : gains.shape[0]]
    at = 0
    pieces = []
    for size in (rows_d, rows_d, HEAD_SIZE // N, HEAD_SIZE // N):
        pieces.append(full_gains[:, at : at + size].reshape(-1).astype(f32))
        at += size
    full_pre, full_post, full_qgain, full_kgain = pieces
    out_blocks = out_columns.reshape(S, qd, D // S)
    out_rows = [lax.dynamic_index_in_dim(out_blocks, Q, 0, False)]
    for r in range(1, S):
        out_rows.append(swap(lax.dynamic_index_in_dim(out_blocks, Q ^ r, 0, False), r))
    full_out = order_seq(jnp.stack(out_rows)).transpose(1, 0, 2).reshape(qd, D)

    def own_columns(weight):
        return lax.dynamic_index_in_dim(
            weight.reshape(rows_d, N, S, piece), Q, 2, False
        ).reshape(rows_d, FQ)

    both_columns = jnp.concatenate([own_columns(gate_weight), own_columns(up_weight)], axis=1)
    full_both = lax.all_gather(both_columns, "shard", axis=0, tiled=True)
    full_down = lax.all_gather(
        lax.dynamic_slice_in_dim(down_weight, Q * piece, piece, 0), "shard", axis=0, tiled=True
    )

    all_tokens = gather_rows(tokens[0])
    cot = cotangent[0]
    all_cot = gather_rows(cot)
    wide = all_tokens.astype(f32)
    root_in = inverse_root(wide)
    scaled_in = wide * root_in
    normed_in = (scaled_in * full_pre).astype(bf16)
    projected = dot(normed_in, full_qkv)
    query_proj = projected[:, :qd].reshape(L, -1, HEAD_SIZE)
    key_proj = projected[:, qd : qd + kd].reshape(L, -1, HEAD_SIZE)
    values = projected[:, qd + kd :].astype(bf16).reshape(L, -1, HEAD_SIZE)
    query_root = inverse_root(query_proj)
    key_root = inverse_root(key_proj)
    queries = rotate(query_proj * query_root * full_qgain, cosine, sine).astype(bf16)
    keys = rotate(key_proj * key_root * full_kgain, cosine, sine).astype(bf16)
    queries = queries.reshape(L, -1, GROUP, HEAD_SIZE)
    scale = HEAD_SIZE ** (-0.5)
    scores = jnp.einsum("qngd,knd->ngqk", queries, keys, preferred_element_type=f32) * scale
    scores = jnp.where(allowed, scores, masked_score)
    probs = jax.nn.softmax(scores, axis=-1)
    attended = (
        jnp.einsum("ngqk,knd->qngd", probs.astype(bf16), values, preferred_element_type=f32)
        .astype(bf16)
        .reshape(L, qd)
    )
    local = tokens[0].astype(f32)
    middle = local + scatter_seq(
        lambda first, count: dot(attended[first : first + count], full_out)
    )

    root_mid = inverse_root(middle)
    scaled_mid = middle * root_mid
    normed_mid = gather_rows((scaled_mid * full_post).astype(bf16))
    both = dot(normed_mid, full_both)
    gate, upper = both[:, :FQ], both[:, FQ:]
    sigmoid = jax.nn.sigmoid(gate)
    swish = gate * sigmoid
    hidden = (swish * upper).astype(bf16)
    term_down = t_times(hidden, all_cot)
    shard_down = lax.psum_scatter(
        term_down.astype(bf16), "shard", scatter_dimension=0, tiled=True
    )
    grad_hidden = times_t(all_cot, full_down)
    grad_both = jnp.concatenate(
        [
            (grad_hidden * upper * (sigmoid * (1.0 + gate * (1.0 - sigmoid)))).astype(bf16),
            (grad_hidden * swish).astype(bf16),
        ],
        axis=1,
    )
    grad_nmid = scatter_seq(
        lambda first, count: times_t(grad_both[first : first + count], full_both)
    )
    term_both = t_times(normed_mid, grad_both)
    shard_both = lax.psum_scatter(
        term_both.astype(bf16), "shard", scatter_dimension=0, tiled=True
    )
    output = middle + scatter_seq(
        lambda first, count: dot(hidden[first : first + count], full_down)
    )
    term_post = jnp.sum(grad_nmid * scaled_mid, axis=0)
    grad_middle = cot.astype(f32) + norm_back(grad_nmid * full_post, middle, root_mid)

    grad_branch = gather_rows(grad_middle.astype(bf16))
    grad_attended = times_t(grad_branch, full_out).astype(bf16)
    term_out = t_times(attended, grad_branch).astype(bf16)
    grad_heads = grad_attended.reshape(L, -1, GROUP, HEAD_SIZE)
    delta = jnp.sum(
        grad_heads.astype(f32) * attended.reshape(grad_heads.shape).astype(f32), axis=-1
    ).transpose(1, 2, 0)
    grad_probs = jnp.einsum("qngd,knd->ngqk", grad_heads, values, preferred_element_type=f32)
    grad_scores = (probs * (grad_probs - delta[..., None])).astype(bf16)
    grad_queries = (
        jnp.einsum("ngqk,knd->qngd", grad_scores, keys, preferred_element_type=f32) * scale
    ).astype(bf16)
    grad_keys = (
        jnp.einsum("ngqk,qngd->knd", grad_scores, queries, preferred_element_type=f32) * scale
    ).astype(bf16)
    grad_values = jnp.einsum(
        "ngqk,qngd->knd", probs.astype(bf16), grad_heads, preferred_element_type=f32
    ).astype(bf16)
    grad_qnorm = rotate_back(
        grad_queries.reshape(L, -1, HEAD_SIZE).astype(f32), cosine, sine
    )
    grad_knorm = rotate_back(grad_keys.astype(f32), cosine, sine)
    term_qgain = jnp.sum(grad_qnorm * query_proj * query_root, axis=(0, 1))
    term_kgain = jnp.sum(grad_knorm * key_proj * key_root, axis=(0, 1))
    grad_qproj = norm_back(grad_qnorm * full_qgain, query_proj, query_root).astype(bf16)
    grad_kproj = norm_back(grad_knorm * full_kgain, key_proj, key_root).astype(bf16)
    grad_proj = jnp.concatenate(
        [grad_qproj.reshape(L, qd), grad_kproj.reshape(L, kd), grad_values.reshape(L, kd)], axis=1
    )
    term_qkv = t_times(normed_in, grad_proj).astype(bf16)
    partial_nin = times_t(grad_proj, full_qkv)
    term_pre = jnp.sum(partial_nin * scaled_in, axis=0)
    grad_nin = scatter_seq(lambda first, count: partial_nin[first : first + count])
    grad_tokens = grad_middle + norm_back(grad_nin * full_pre, local, root_in[:T])

    out_parts = term_out.reshape(qd, S, D // S).transpose(1, 0, 2)
    parts = [lax.dynamic_index_in_dim(out_parts, Q, 0, False)]
    for r in range(1, S):
        parts.append(swap(lax.dynamic_index_in_dim(out_parts, Q ^ r, 0, False), r))
    term_columns = order_seq(jnp.stack(parts)).reshape(D, D // S)
    term_gains = jnp.concatenate(
        [
            term_pre.reshape(N, rows_d),
            term_post.reshape(N, rows_d),
            term_qgain.reshape(N, -1),
            term_kgain.reshape(N, -1),
        ],
        axis=1,
    ).astype(bf16)
    term_packed = jnp.concatenate([term_qkv, term_columns], axis=1).reshape(N, rows_d, -1)
    gains_part = jnp.pad(
        term_gains[:, None, :], ((0, 0), (0, 15), (0, term_packed.shape[2] - term_gains.shape[1]))
    )
    shard_packed = lax.psum_scatter(
        jnp.concatenate([term_packed, gains_part], axis=1), "shard", scatter_dimension=0
    )

    down_all = order_seq(gather_seq(shard_down))
    grad_down = down_all.reshape(-1, D).astype(f32)
    both_all = order_seq(gather_seq(shard_both)).reshape(S, rows_d, 2, N, piece)
    both_all = both_all.transpose(2, 1, 3, 0, 4).reshape(2, rows_d, FF).astype(f32)
    packed_all = order_seq(gather_seq(shard_packed))
    gains_all = jnp.sum(packed_all[:, rows_d, :].astype(f32), axis=0)

    def columns(first, count):
        return (
            packed_all[:, :rows_d, first : first + count]
            .transpose(1, 0, 2)
            .reshape(rows_d, S * count)
            .astype(f32)
        )

    small = HEAD_SIZE // N
    return (
        output.astype(bf16)[None],
        grad_tokens[None],
        gains_all[:rows_d],
        columns(0, qd),
        columns(qd, kd),
        columns(qd + kd, kd),
        gains_all[2 * rows_d : 2 * rows_d + small],
        gains_all[2 * rows_d + small : 2 * rows_d + 2 * small],
        columns(width, D // S),
        gains_all[rows_d : 2 * rows_d],
        both_all[0],
        both_all[1],
        grad_down,
    )


def solution(mesh):
    row, vector, matrix = P("shard", "seq", None), P("shard"), P("shard", None)
    return jax.shard_map(
        per_device,
        mesh=mesh,
        in_specs=(
            row,
            matrix,
            vector,
            matrix,
            matrix,
            matrix,
            vector,
            vector,
            matrix,
            vector,
            matrix,
            matrix,
            matrix,
            row,
        ),
        out_specs=(
            row,
            row,
            vector,
            matrix,
            matrix,
            matrix,
            vector,
            vector,
            matrix,
            vector,
            matrix,
            matrix,
            matrix,
        ),
        check_vma=False,
    )
```

time: 1620 us -> 554 us (0.34)
  waiting for transfers between devices: 1240 us -> 308 us
  blocking collectives: 107 us -> 0 us
  matrix products: 127 us -> 79.7 us
    reduce_scatter x7 -> x3, waiting for transfers between devices: 715 us -> 146 us  [the longest x1 91.8 us: per_device(): lax.psum_scatter(term_both.astype(bf16), 'shard', scatter_dimension=0, ti...]
    all_gather x7 -> x3, waiting for transfers between devices: 458 us -> 64.1 us  [the longest x1 36.5 us: per_device(): lax.all_gather(lax.dynamic_slice_in_dim(down_weight, Q * piece, piece, 0)...]
    ppermute x0 -> x32, waiting for transfers between devices: none -> 97 us  [swap(): return lax.ppermute(x, 'seq', [(i, i ^ step) for i in range(S)])]
    psum x1 -> x0, waiting for transfers between devices: 50.4 us -> none  [per_device(): lax.psum(shard_query.astype(jnp.bfloat16), 'seq').astype(jnp.float32)]
    all_gather x2 -> x0, blocking collectives: 40.4 us -> none  [the longest x1 22.3 us: per_device(): lax.all_gather(pre_gain, 'shard', axis=0, tiled=True)]
    dot_general x28 -> x11, matrix products: 72.2 us -> 31.8 us  [the longest x6 15.8 us: dot(): return jnp.dot(left, right, preferred_element_type=f32)]
    unnamed x2 -> x0, blocking collectives: 36.9 us -> none
    all_to_all x2 -> x0, blocking collectives: 22.9 us -> none  [the longest x1 11.5 us: per_device(): lax.all_to_all(query_back, 'seq', split_axis=0, concat_axis=1, tiled=True)]
  transfers between devices with their start and end apart: 19 -> 38, of which waited for: 15 -> 17; matrix products, arithmetic and copies ran while one was open for 7% -> 27% of each run, Pallas kernels for 0% -> 0%
where the time goes in v1:
time: 554 us; the launch traced here: 545 us
  waiting for transfers between devices  308 us (56%)
  matrix products  79.7 us (14%)
  local copies, waits for them, and re-layouts  63.7 us (11%)
  other arithmetic  55 us (10%)
  starting transfers between devices  22.8 us (4%)
  between operations  16 us (3%)
    ppermute x32, waiting for transfers between devices, swap(): return lax.ppermute(x, 'seq', [(i, i ^ step) for i in range(S)])  97 us
    reduce_scatter x1, waiting for transfers between devices, per_device(): lax.psum_scatter(term_both.astype(bf16), 'shard', scatter_dimension=0, ti...  91.8 us
    reduce_scatter x1, waiting for transfers between devices, per_device(): lax.psum_scatter(jnp.concatenate([term_packed, gains_part], axis=1), 'sha...  48.9 us
    all_gather x1, waiting for transfers between devices, per_device(): lax.all_gather(lax.dynamic_slice_in_dim(down_weight, Q * piece, piece, 0)...  36.5 us
    unnamed x144, local copies, waits for them, and re-layouts  28.2 us
    all_gather x1, waiting for transfers between devices, per_device(): lax.all_gather(jnp.concatenate([own, gains_rows], axis=0), 'shard', axis=0)  27.6 us
    ppermute x32, starting transfers between devices, swap(): return lax.ppermute(x, 'seq', [(i, i ^ step) for i in range(S)])  22.5 us
    dot_general x4, matrix products, t_times(): lax.dot_general(left, right, (((0,), (0,)), ((), ())), preferred_element_...  18.6 us
  transfers between devices with their start and end apart: 38, of which 17 were waited for; matrix products, arithmetic and copies ran while one was open for 27% of the time, Pallas kernels for 0%

profile of v1, /device:TPU:0, one launch (start us, length us, event | category | flops | bytes accessed | tf_op | source)
XLA Modules:
  0.0 544.8 jit_solution(13613377528875506836)
XLA Ops:
  10.6 3.0 collective-permute-start
  20.5 5.2 collective-permute-done
  31.8 27.6 %all-gather.9.cloned.1.call-done = bf16[1152,768]{1,0:T(8,128)(2,1)} async-done(((bf16[144,768]{1,0:T(8,128)(2,1)}), bf16[1152,768]{1,0:T(8,128)(2,1)}) %all-gather.9.cloned.1.call-update) | async-done | bytes 1769488 | tf_op jit(solution)/shard_map/all_gather | solution.py:152
  78.8 11.2 %fusion.106 = (f32[2,2,1024]{2,1,0:T(2,128)S(1)}, f32[2,2,1024,1024]{2,3,1,0:T(8,128)}) fusion(pred[1024,1024]{0,1:T(8,128)(4,1)} %compare_and_fusion, bf16[1024,2,64,1]{0,2,3,1:T(8,128)(2,1)} %fusion.76, bf16[1024,2,2,64]{0,3,2,1:T(8,128)(2,1)S(1)} %fusion.50), kind=kOutput, calls=%fused_computation.276 | convolution fusion | flops 553649152 | bytes 18628608 | tf_op jit(solution)/shard_map/sub | solution.py:198
  90.0 7.7 %fusion.7 = bf16[2,2,1024,1024]{2,3,1,0:T(8,128)(2,1)S(1)} fusion(f32[2,2,1024,1024]{2,3,1,0:T(8,128)} %get-tuple-element.193, f32[2,2,1024]{2,1,0:T(2,128)S(1)} %get-tuple-element.192), kind=kLoop, calls=%fused_computation.11 | loop fusion | flops 8388608 | bytes 25182208 | tf_op jit(solution)/shard_map/convert_element_type | solution.py:200
  109.6 12.1 %collective-permute-done.7 = bf16[256,1024]{1,0:T(8,128)(2,1)} collective-permute-done((bf16[256,1024]{1,0:T(8,128)(2,1)}, bf16[256,1024]{1,0:T(8,128)(2,1)}, u32[]{:S(2)}, u32[]{:S(2)}) %collective-permute-start.7) | collective-permute-done | bytes 524320 | tf_op jit(solution)/shard_map/ppermute | solution.py:104
  125.4 7.5 %collective-permute-done.13 = bf16[1,256,1024]{2,1,0:T(8,128)(2,1)S(1)} collective-permute-done((bf16[1,256,1024]{2,1,0:T(8,128)(2,1)S(1)}, bf16[1,256,1024]{2,1,0:T(8,128)(2,1)S(1)}, u32[]{:S(2)}, u32[]{:S(2)}) %collective-permute-start.13) | collective-permute-done | bytes 524320 | tf_op jit(solution)/shard_map/ppermute | solution.py:104
  133.1 10.4 %collective-permute-done.8 = bf16[1,256,1024]{2,1,0:T(8,128)(2,1)S(1)} collective-permute-done((bf16[1,256,1024]{2,1,0:T(8,128)(2,1)S(1)}, bf16[1,256,1024]{2,1,0:T(8,128)(2,1)S(1)}, u32[]{:S(2)}, u32[]{:S(2)}) %collective-permute-start.8) | collective-permute-done | bytes 524320 | tf_op jit(solution)/shard_map/ppermute | solution.py:104
  148.1 10.5 %fusion.110 = f32[1024,2304]{1,0:T(8,128)} fusion(bf16[1024,1024]{1,0:T(8,128)(2,1)} %bitcast.355, bf16[1024,2304]{0,1:T(8,128)(2,1)} %all-gather.5.cloned.1.call-done), kind=kOutput, calls=%fused_computation.280 | convolution fusion | flops 4831838208 | bytes 16252928 | tf_op jit(solution)/shard_map/dot_general | solution.py:23
  158.6 36.5 %all-gather.7.cloned.1.call-done = bf16[1152,1024]{1,0:T(8,128)(2,1)} async-done(((bf16[144,1024]{1,0:T(8,128)(2,1)}), bf16[1152,1024]{1,0:T(8,128)(2,1)}) %all-gather.7.cloned.1.call-update) | async-done | bytes 2359312 | tf_op jit(solution)/shard_map/all_gather | solution.py:175
  195.1 7.9 %multiply_convert_fusion = (bf16[1024,1152]{1,0:T(8,128)(2,1)S(1)}, bf16[1024,1152]{1,0:T(8,128)(2,1)S(1)}, bf16[1024,1152]{1,0:T(8,128)(2,1)S(1)}) fusion(f32[1024,2304]{1,0:T(8,128)} %fusion.110, bf16[1024,1024]{1,0:T(8,128)(2,1)S(1)} %bitcast.358, bf16[1152,1024]{1,0:T(8,128)(2,1)} %all-gather.7.cloned.1.call-done), kind=kOutput, calls=%fused_computation.18 | convolution fusion | flops 2433613824 | bytes 20971520 | tf_op jit(solution)/shard_map/dot_general | solution.py:27
  204.8 3.1 copy-done.57
  210.7 2.6 fusion.11
  218.1 10.8 %collective-permute-done.17 = bf16[256,1024]{1,0:T(8,128)(2,1)S(1)} collective-permute-done((bf16[256,1024]{1,0:T(8,128)(2,1)S(1)}, bf16[256,1024]{1,0:T(8,128)(2,1)S(1)}, u32[]{:S(2)}, u32[]{:S(2)}) %collective-permute-start.17) | collective-permute-done | bytes 524320 | tf_op jit(solution)/shard_map/ppermute | solution.py:104
  229.3 9.9 %collective-permute-done.12 = bf16[256,1024]{1,0:T(8,128)(2,1)S(1)} collective-permute-done((bf16[256,1024]{1,0:T(8,128)(2,1)S(1)}, bf16[256,1024]{1,0:T(8,128)(2,1)S(1)}, u32[]{:S(2)}, u32[]{:S(2)}) %collective-permute-start.12) | collective-permute-done | bytes 524320 | tf_op jit(solution)/shard_map/ppermute | solution.py:104
  242.1 11.5 %collective-permute-done.18 = bf16[1,256,1024]{2,1,0:T(8,128)(2,1)S(1)} collective-permute-done((bf16[1,256,1024]{2,1,0:T(8,128)(2,1)S(1)}, bf16[1,256,1024]{2,1,0:T(8,128)(2,1)S(1)}, u32[]{:S(2)}, u32[]{:S(2)}) %collective-permute-start.18) | collective-permute-done | bytes 524320 | tf_op jit(solution)/shard_map/ppermute | solution.py:104
  254.0 6.3 %convolution_convert_fusion.1 = bf16[1152,1024]{1,0:T(8,128)(2,1)} fusion(bf16[1024,1152]{1,0:T(8,128)(2,1)} %copy-done.59, bf16[1024,1024]{1,0:T(8,128)(2,1)} %bitcast.357), kind=kOutput, calls=%fused_computation.29 | convolution fusion | flops 2417098752 | bytes 6815744 | tf_op jit(solution)/shard_map/dot_general | solution.py:31
  264.1 7.6 %fusion.2 = bf16[2,2,1024,1024]{2,3,1,0:T(8,128)(2,1)S(1)} fusion(f32[2,2,1024]{2,1,0:T(2,128)S(1)} %bitcast.417, f32[2,2,1024,1024]{2,3,1,0:T(8,128)} %get-tuple-element.193, f32[2,2,1024]{2,1,0:T(2,128)S(1)} %copy-done.51, bf16[1024,2,64,1]{0,2,3,1:T(8,128)(2,1)S(1)} %bitcast.376, bf16[1024,2,2,64]{0,3,2,1:T(8,128)(2,1)S(1)} %bitcast.389), kind=kOutput, calls=%fused_computation.3 | convolution fusion | flops 553648128 | bytes 25985024 | tf_op jit(solution)/shard_map/qngd,knd->ngqk/dot_general | solution.py:249
  290.1 2.7 broadcast_multiply_fusion
  294.1 2.7 fusion.25
  296.8 4.1 multiply_reduce_fusion
  305.3 9.5 %convolution_convert_fusion = bf16[1024,2304]{1,0:T(8,128)(2,1)} fusion(bf16[1024,1024]{1,0:T(8,128)(2,1)} %bitcast.356, bf16[1024,1152]{1,0:T(8,128)(2,1)} %copy-done.60, bf16[1024,1152]{1,0:T(8,128)(2,1)} %copy-done.61), kind=kOutput, calls=%fused_computation.17 | convolution fusion | flops 4843634688 | bytes 11534336 | tf_op jit(solution)/shard_map/dot_general | solution.py:31
  322.5 5.7 %reduce-scatter.8.cloned.1.call-done = bf16[144,1024]{1,0:T(8,128)(2,1)} async-done(((bf16[1152,1024]{1,0:T(8,128)(2,1)}), bf16[144,1024]{1,0:T(8,128)(2,1)}) %reduce-scatter.8.cloned.1.call-update) | async-done | bytes 294928 | tf_op jit(solution)/shard_map/reduce_scatter | solution.py:218
  329.6 11.9 %collective-permute-done.30 = bf16[1,144,1024]{2,1,0:T(8,128)(2,1)S(1)} collective-permute-done((bf16[1,144,1024]{2,1,0:T(8,128)(2,1)}, bf16[1,144,1024]{2,1,0:T(8,128)(2,1)S(1)}, u32[]{:S(2)}, u32[]{:S(2)}) %collective-permute-start.30) | collective-permute-done | bytes 294944 | tf_op jit(solution)/shard_map/ppermute | solution.py:104
  345.0 2.6 fusion.36
  347.7 48.9 %reduce-scatter.4.cloned.1.call-done = bf16[1,144,768]{2,1,0:T(8,128)(2,1)} async-done(((bf16[8,144,768]{2,1,0:T(8,128)(2,1)}), bf16[1,144,768]{2,1,0:T(8,128)(2,1)}) %reduce-scatter.4.cloned.1.call-update) | async-done | bytes 221200 | tf_op jit(solution)/shard_map/reduce_scatter | solution.py:295
  399.5 3.2 collective-permute-done.26
  402.9 91.8 %reduce-scatter.6.cloned.1.call-done = bf16[128,2304]{1,0:T(8,128)(2,1)} async-done(((bf16[1024,2304]{1,0:T(8,128)(2,1)}), bf16[128,2304]{1,0:T(8,128)(2,1)}) %reduce-scatter.6.cloned.1.call-update) | async-done | bytes 589840 | tf_op jit(solution)/shard_map/reduce_scatter | solution.py:233
  498.2 11.7 %collective-permute-done.28 = bf16[1,128,2304]{2,1,0:T(8,128)(2,1)S(1)} collective-permute-done((bf16[1,128,2304]{2,1,0:T(8,128)(2,1)}, bf16[1,128,2304]{2,1,0:T(8,128)(2,1)S(1)}, u32[]{:S(2)}, u32[]{:S(2)}) %collective-permute-start.28) | collective-permute-done | bytes 589856 | tf_op jit(solution)/shard_map/ppermute | solution.py:104
  518.8 2.6 maximum_convert_fusion
  521.3 6.1 %copy.178 = f32[4,128,2304]{1,2,0:T(8,128)} copy(f32[4,128,2304]{2,1,0:T(8,128)} %maximum_convert_fusion) | data formatting | bytes 9437184 | tf_op jit(solution)/shard_map/convert_element_type | solution.py:302
  527.4 4.1 fusion.98
  (348 shorter events, 129.7 us)
Async XLA Ops:
  7.2 52.2 %all-gather.9.cloned.1.call-start = ((), (), s32[]{:S(2)}) async-start(), calls=%async_computation.8 | async-start | bytes 1990656 | tf_op jit(solution)/shard_map/all_gather | solution.py:152
  10.5 137.6 %all-gather.5.cloned.1.call-start = ((), (), s32[]{:S(2)}) async-start(), calls=%async_computation.3 | async-start | bytes 5308416 | tf_op jit(solution)/shard_map/all_gather | solution.py:174
  10.6 15.2 %collective-permute-start = (bf16[1,256,1024]{2,1,0:T(8,128)(2,1)}, bf16[1,256,1024]{2,1,0:T(8,128)(2,1)S(1)}, u32[]{:S(2)}, u32[]{:S(2)}) collective-permute-start(bf16[1,256,1024]{2,1,0:T(8,128)(2,1)} %param.16), channel_id=1, source_target_pairs={{0,16},{8,24},{16,0},{24,8},{1,17},{9,25},{17,1},{25,9},{2,18},{10... | collective-permute-start | bytes 1572872 | tf_op jit(solution)/shard_map/ppermute | solution.py:104
  20.4 174.7 %all-gather.7.cloned.1.call-start = ((), (), s32[]{:S(2)}) async-start(), calls=%async_computation.4 | async-start | bytes 2654208 | tf_op jit(solution)/shard_map/all_gather | solution.py:175
  72.6 28.4 %collective-permute-start.2 = (bf16[256,256]{1,0:T(8,128)(2,1)}, bf16[256,256]{1,0:T(8,128)(2,1)}, u32[]{:S(2)}, u32[]{:S(2)}) collective-permute-start(bf16[256,256]{1,0:T(8,128)(2,1)} %get-tuple-element.167), channel_id=1, source_target_pairs={{0,8},{8,0},{16,24},{24,16},{1,9},{9,1},{17,25},{25,17},{2,10},{10... | collective-permute-start | bytes 393224 | tf_op jit(solution)/shard_map/ppermute | solution.py:104
  72.6 28.4 %collective-permute-start.3 = (bf16[256,256]{1,0:T(8,128)(2,1)}, bf16[256,256]{1,0:T(8,128)(2,1)}, u32[]{:S(2)}, u32[]{:S(2)}) collective-permute-start(bf16[256,256]{1,0:T(8,128)(2,1)} %get-tuple-element.166), channel_id=1, source_target_pairs={{0,16},{8,24},{16,0},{24,8},{1,17},{9,25},{17,1},{25,9},{2,18},{10... | collective-permute-start | bytes 393224 | tf_op jit(solution)/shard_map/ppermute | solution.py:104
  74.2 26.8 %collective-permute-start.4 = (bf16[256,256]{1,0:T(8,128)(2,1)}, bf16[256,256]{1,0:T(8,128)(2,1)}, u32[]{:S(2)}, u32[]{:S(2)}) collective-permute-start(bf16[256,256]{1,0:T(8,128)(2,1)} %get-tuple-element.165), channel_id=1, source_target_pairs={{0,24},{8,16},{16,8},{24,0},{1,25},{9,17},{17,9},{25,1},{2,26},{10... | collective-permute-start | bytes 393224 | tf_op jit(solution)/shard_map/ppermute | solution.py:104
  106.7 15.1 %collective-permute-start.7 = (bf16[256,1024]{1,0:T(8,128)(2,1)}, bf16[256,1024]{1,0:T(8,128)(2,1)}, u32[]{:S(2)}, u32[]{:S(2)}) collective-permute-start(bf16[256,1024]{1,0:T(8,128)(2,1)} %fusion.47), channel_id=1, source_target_pairs={{0,16},{8,24},{16,0},{24,8},{1,17},{9,25},{17,1},{25,9},{2,18},{10... | collective-permute-start | bytes 1572872 | tf_op jit(solution)/shard_map/ppermute | solution.py:104
  108.9 219.2 %reduce-scatter.8.cloned.1.call-start = ((), (), s32[]{:S(2)}) async-start(), calls=%async_computation.7 | async-start | bytes 2654208 | tf_op jit(solution)/shard_map/reduce_scatter | solution.py:218
  109.0 23.9 %collective-permute-start.13 = (bf16[1,256,1024]{2,1,0:T(8,128)(2,1)S(1)}, bf16[1,256,1024]{2,1,0:T(8,128)(2,1)S(1)}, u32[]{:S(2)}, u32[]{:S(2)}) collective-permute-start(bf16[1,256,1024]{2,1,0:T(8,128)(2,1)S(1)} %copy-done.25), channel_id=1, source_target_pairs={{0,16},{8,24},{16,0},{24,8},{1,17},{9,25},{17,1},{25,9},{2,18},{10... | collective-permute-start | bytes 1572872 | tf_op jit(solution)/shard_map/ppermute | solution.py:104
  123.8 19.7 %collective-permute-start.8 = (bf16[1,256,1024]{2,1,0:T(8,128)(2,1)S(1)}, bf16[1,256,1024]{2,1,0:T(8,128)(2,1)S(1)}, u32[]{:S(2)}, u32[]{:S(2)}) collective-permute-start(bf16[1,256,1024]{2,1,0:T(8,128)(2,1)S(1)} %get-tuple-element.124), channel_id=1, source_target_pairs={{0,16},{8,24},{16,0},{24,8},{1,17},{9,25},{17,1},{25,9},{2,18},{10... | collective-permute-start | bytes 1572872 | tf_op jit(solution)/shard_map/ppermute | solution.py:104
  133.0 10.7 %collective-permute-start.14 = (bf16[2,256,1024]{2,1,0:T(8,128)(2,1)S(1)}, bf16[2,256,1024]{2,1,0:T(8,128)(2,1)S(1)}, u32[]{:S(2)}, u32[]{:S(2)}) collective-permute-start(bf16[2,256,1024]{2,1,0:T(8,128)(2,1)S(1)} %get-tuple-element.133), channel_id=1, source_target_pairs={{0,8},{8,0},{16,24},{24,16},{1,9},{9,1},{17,25},{25,17},{2,10},{10... | collective-permute-start | bytes 3145736 | tf_op jit(solution)/shard_map/ppermute | solution.py:104
  204.7 12.6 %collective-permute-start.11 = (bf16[256,1024]{1,0:T(8,128)(2,1)S(1)}, bf16[256,1024]{1,0:T(8,128)(2,1)S(1)}, u32[]{:S(2)}, u32[]{:S(2)}) collective-permute-start(bf16[256,1024]{1,0:T(8,128)(2,1)S(1)} %slice.409), channel_id=1, source_target_pairs={{0,8},{8,0},{16,24},{24,16},{1,9},{9,1},{17,25},{25,17},{2,10},{10... | collective-permute-start | bytes 1572872 | tf_op jit(solution)/shard_map/ppermute | solution.py:104
  213.4 4.7 collective-permute-start.15
  214.1 14.8 %collective-permute-start.17 = (bf16[256,1024]{1,0:T(8,128)(2,1)S(1)}, bf16[256,1024]{1,0:T(8,128)(2,1)S(1)}, u32[]{:S(2)}, u32[]{:S(2)}) collective-permute-start(bf16[256,1024]{1,0:T(8,128)(2,1)S(1)} %fusion.41), channel_id=1, source_target_pairs={{0,16},{8,24},{16,0},{24,8},{1,17},{9,25},{17,1},{25,9},{2,18},{10... | collective-permute-start | bytes 1572872 | tf_op jit(solution)/shard_map/ppermute | solution.py:104
  217.2 12.1 %collective-permute-start.10 = (bf16[256,1024]{1,0:T(8,128)(2,1)S(1)}, bf16[256,1024]{1,0:T(8,128)(2,1)S(1)}, u32[]{:S(2)}, u32[]{:S(2)}) collective-permute-start(bf16[256,1024]{1,0:T(8,128)(2,1)S(1)} %slice.410), channel_id=1, source_target_pairs={{0,8},{8,0},{16,24},{24,16},{1,9},{9,1},{17,25},{25,17},{2,10},{10... | collective-permute-start | bytes 1572872 | tf_op jit(solution)/shard_map/ppermute | solution.py:104
  217.5 21.7 %collective-permute-start.12 = (bf16[256,1024]{1,0:T(8,128)(2,1)S(1)}, bf16[256,1024]{1,0:T(8,128)(2,1)S(1)}, u32[]{:S(2)}, u32[]{:S(2)}) collective-permute-start(bf16[256,1024]{1,0:T(8,128)(2,1)S(1)} %fusion.43), channel_id=1, source_target_pairs={{0,16},{8,24},{16,0},{24,8},{1,17},{9,25},{17,1},{25,9},{2,18},{10... | collective-permute-start | bytes 1572872 | tf_op jit(solution)/shard_map/ppermute | solution.py:104
  240.6 13.1 %collective-permute-start.18 = (bf16[1,256,1024]{2,1,0:T(8,128)(2,1)S(1)}, bf16[1,256,1024]{2,1,0:T(8,128)(2,1)S(1)}, u32[]{:S(2)}, u32[]{:S(2)}) collective-permute-start(bf16[1,256,1024]{2,1,0:T(8,128)(2,1)S(1)} %convert_bitcast_fusion.4), channel_id=1, source_target_pairs={{0,16},{8,24},{16,0},{24,8},{1,17},{9,25},{17,1},{25,9},{2,18},{10... | collective-permute-start | bytes 1572872 | tf_op jit(solution)/shard_map/ppermute | solution.py:104
  253.8 6.6 %collective-permute-start.19 = (bf16[2,256,1024]{2,1,0:T(8,128)(2,1)S(1)}, bf16[2,256,1024]{2,1,0:T(8,128)(2,1)}, u32[]{:S(2)}, u32[]{:S(2)}) collective-permute-start(bf16[2,256,1024]{2,1,0:T(8,128)(2,1)S(1)} %get-tuple-element.130), channel_id=1, source_target_pairs={{0,8},{8,0},{16,24},{24,16},{1,9},{9,1},{17,25},{25,17},{2,10},{10... | collective-permute-start | bytes 3145736 | tf_op jit(solution)/shard_map/ppermute | solution.py:104
  260.4 136.3 %reduce-scatter.4.cloned.1.call-start = ((), (), s32[]{:S(2)}) async-start(), calls=%async_computation.5 | async-start | bytes 1990656 | tf_op jit(solution)/shard_map/reduce_scatter | solution.py:295
  281.8 20.9 %collective-permute-start.25 = (bf16[256,256]{1,0:T(8,128)(2,1)}, bf16[256,256]{1,0:T(8,128)(2,1)}, u32[]{:S(2)}, u32[]{:S(2)}) collective-permute-start(bf16[256,256]{1,0:T(8,128)(2,1)} %bitcast.330), channel_id=1, source_target_pairs={{0,24},{8,16},{16,8},{24,0},{1,25},{9,17},{17,9},{25,1},{2,26},{10... | collective-permute-start | bytes 393224 | tf_op jit(solution)/shard_map/ppermute | solution.py:104
  284.0 18.6 %collective-permute-start.23 = (bf16[256,256]{1,0:T(8,128)(2,1)}, bf16[256,256]{1,0:T(8,128)(2,1)}, u32[]{:S(2)}, u32[]{:S(2)}) collective-permute-start(bf16[256,256]{1,0:T(8,128)(2,1)} %bitcast.332), channel_id=1, source_target_pairs={{0,8},{8,0},{16,24},{24,16},{1,9},{9,1},{17,25},{25,17},{2,10},{10... | collective-permute-start | bytes 393224 | tf_op jit(solution)/shard_map/ppermute | solution.py:104
  284.7 17.9 %collective-permute-start.24 = (bf16[256,256]{1,0:T(8,128)(2,1)}, bf16[256,256]{1,0:T(8,128)(2,1)}, u32[]{:S(2)}, u32[]{:S(2)}) collective-permute-start(bf16[256,256]{1,0:T(8,128)(2,1)} %bitcast.331), channel_id=1, source_target_pairs={{0,16},{8,24},{16,0},{24,8},{1,17},{9,25},{17,1},{25,9},{2,18},{10... | collective-permute-start | bytes 393224 | tf_op jit(solution)/shard_map/ppermute | solution.py:104
  305.3 189.4 %reduce-scatter.6.cloned.1.call-start = ((), (), s32[]{:S(2)}) async-start(), calls=%async_computation.6 | async-start | bytes 5308416 | tf_op jit(solution)/shard_map/reduce_scatter | solution.py:233
  317.1 26.3 %collective-permute-start.20 = (bf16[256,1024]{1,0:T(8,128)(2,1)}, bf16[256,1024]{1,0:T(8,128)(2,1)S(1)}, u32[]{:S(2)}, u32[]{:S(2)}) collective-permute-start(bf16[256,1024]{1,0:T(8,128)(2,1)} %get-tuple-element.115), channel_id=1, source_target_pairs={{0,8},{8,0},{16,24},{24,16},{1,9},{9,1},{17,25},{25,17},{2,10},{10... | collective-permute-start | bytes 1572872 | tf_op jit(solution)/shard_map/ppermute | solution.py:104
  321.0 22.4 %collective-permute-start.22 = (bf16[256,1024]{1,0:T(8,128)(2,1)}, bf16[256,1024]{1,0:T(8,128)(2,1)S(1)}, u32[]{:S(2)}, u32[]{:S(2)}) collective-permute-start(bf16[256,1024]{1,0:T(8,128)(2,1)} %fusion.38), channel_id=1, source_target_pairs={{0,16},{8,24},{16,0},{24,8},{1,17},{9,25},{17,1},{25,9},{2,18},{10... | collective-permute-start | bytes 1572872 | tf_op jit(solution)/shard_map/ppermute | solution.py:104
  328.2 13.4 %collective-permute-start.30 = (bf16[1,144,1024]{2,1,0:T(8,128)(2,1)}, bf16[1,144,1024]{2,1,0:T(8,128)(2,1)S(1)}, u32[]{:S(2)}, u32[]{:S(2)}) collective-permute-start(bf16[1,144,1024]{2,1,0:T(8,128)(2,1)} %bitcast.397), channel_id=1, source_target_pairs={{0,16},{8,24},{16,0},{24,8},{1,17},{9,25},{17,1},{25,9},{2,18},{10... | collective-permute-start | bytes 884744 | tf_op jit(solution)/shard_map/ppermute | solution.py:104
  343.4 54.7 %collective-permute-start.31 = (bf16[2,144,1024]{2,1,0:T(8,128)(2,1)}, bf16[2,144,1024]{2,1,0:T(8,128)(2,1)}, u32[]{:S(2)}, u32[]{:S(2)}) collective-permute-start(bf16[2,144,1024]{2,1,0:T(8,128)(2,1)} %get-tuple-element.147), channel_id=1, source_target_pairs={{0,8},{8,0},{16,24},{24,16},{1,9},{9,1},{17,25},{25,17},{2,10},{10... | collective-permute-start | bytes 1769480 | tf_op jit(solution)/shard_map/ppermute | solution.py:104
  396.6 6.1 %collective-permute-start.26 = (bf16[1,144,768]{2,1,0:T(8,128)(2,1)}, bf16[1,144,768]{2,1,0:T(8,128)(2,1)S(1)}, u32[]{:S(2)}, u32[]{:S(2)}) collective-permute-start(bf16[1,144,768]{2,1,0:T(8,128)(2,1)} %reduce-scatter.4.cloned.1.call-done), channel_id=1, source_target_pairs={{0,16},{8,24},{16,0},{24,8},{1,17},{9,25},{17,1},{25,9},{2,18},{10... | collective-permute-start | bytes 663560 | tf_op jit(solution)/shard_map/ppermute | solution.py:104
  402.8 95.3 %collective-permute-start.27 = (bf16[2,144,768]{2,1,0:T(8,128)(2,1)S(1)}, bf16[2,144,768]{2,1,0:T(8,128)(2,1)S(1)}, u32[]{:S(2)}, u32[]{:S(2)}) collective-permute-start(bf16[2,144,768]{2,1,0:T(8,128)(2,1)S(1)} %get-tuple-element.171), channel_id=1, source_target_pairs={{0,8},{8,0},{16,24},{24,16},{1,9},{9,1},{17,25},{25,17},{2,10},{10... | collective-permute-start | bytes 1327112 | tf_op jit(solution)/shard_map/ppermute | solution.py:104
  494.7 15.2 %collective-permute-start.28 = (bf16[1,128,2304]{2,1,0:T(8,128)(2,1)}, bf16[1,128,2304]{2,1,0:T(8,128)(2,1)S(1)}, u32[]{:S(2)}, u32[]{:S(2)}) collective-permute-start(bf16[1,128,2304]{2,1,0:T(8,128)(2,1)} %bitcast.386), channel_id=1, source_target_pairs={{0,16},{8,24},{16,0},{24,8},{1,17},{9,25},{17,1},{25,9},{2,18},{10... | collective-permute-start | bytes 1769480 | tf_op jit(solution)/shard_map/ppermute | solution.py:104
  511.1 5.8 %collective-permute-start.29 = (bf16[2,128,2304]{2,1,0:T(8,128)(2,1)}, bf16[2,128,2304]{2,1,0:T(8,128)(2,1)}, u32[]{:S(2)}, u32[]{:S(2)}) collective-permute-start(bf16[2,128,2304]{2,1,0:T(8,128)(2,1)} %get-tuple-element.122), channel_id=1, source_target_pairs={{0,8},{8,0},{16,24},{24,16},{1,9},{9,1},{17,25},{25,17},{2,10},{10... | collective-permute-start | bytes 3538952 | tf_op jit(solution)/shard_map/ppermute | solution.py:104
  (72 other events, 624.1 us)
Sparse Core Ops, SparseCore 0:
  10.8 48.5 all-gather.8
  62.0 80.0 all-gather.4
  144.8 50.2 all-gather.6
  260.5 67.6 reduce-scatter.7
  331.5 65.0 reduce-scatter.3
  400.5 94.1 reduce-scatter.5
